TPU v7x, 32 devices: a whole 2x2x4 slice. The times are simulated.
32 devices in a mesh: rows: 8 (over y, x, core), rhs: 4 (over z).
Axes of the slice: x: 2, y: 2, z: 4, core: 2. Of those that a mesh axis runs over, the one named last changes fastest.
Arguments:
- samples: float32 [65536, 16], P(('rows', 'rhs')), may hold values from -5 to 5
- freq_table: float32 [4096, 16], replicated, may hold values from -3 to 3
- feature_seeds: int32 [512], replicated, may hold values from 0 to 4095
- phases: float32 [512], replicated, may hold values from -3.140625 to 3.140625
- treatment_features: bfloat16 [65536, 512], P('rows', 'rhs'), may hold values from -2.5 to 2.5, as said below
Outputs:
- coefficients: float32 [512, 512], replicated
- fitted: float32 [65536, 512], P(('rows', 'rhs'))
Inputs may be any that keep to these rules, and one draw needn't show every extreme that they name: `treatment_features`: treatment features depend on the instrument values.
All inputs are finite; a program needn't handle non-finite values.
Results may differ from a plain program's by a relative error of at most 0.0008.
The roundings to bfloat16 on the way count: a program that leaves them out, or rounds other values in their place, can miss the bound.
Values may be sent and summed in bfloat16 or wider, within the bound.
A program may use at most 64 MiB of HBM per device.

v0:
```python
import jax
import jax.numpy as jnp
from jax import lax
from jax.sharding import PartitionSpec as P

ridge = 0.05


def solve_with(factor, right):
    lower = lax.linalg.triangular_solve(factor, right, left_side=True, lower=True)
    return lax.linalg.triangular_solve(factor, lower, left_side=True, lower=True, transpose_a=True)


def features_of(values, freqs, phases):
    angles = (
        jnp.dot(
            values, freqs.T, precision=lax.Precision.HIGHEST, preferred_element_type=jnp.float32
        )
        + phases
    )
    return (jnp.sqrt(jnp.float32(2.0)) * jnp.cos(angles)).astype(jnp.bfloat16)


def body(samples, freq_table, feature_seeds, phases, treatment_features):
    own_rows = samples.shape[0]
    count = own_rows * lax.axis_size("rows") * lax.axis_size("rhs")
    freqs = freq_table[feature_seeds]
    contract = (((0,), (0,)), ((), ()))
    instruments = features_of(samples, freqs, phases)
    gram_part = lax.dot_general(
        instruments, instruments, contract, preferred_element_type=jnp.float32
    )
    gram = lax.psum(gram_part, ("rows", "rhs")) / count
    gram = gram + ridge * jnp.eye(gram.shape[0], dtype=jnp.float32)
    factor = jnp.linalg.cholesky(gram)
    targets = lax.all_to_all(treatment_features, "rhs", split_axis=0, concat_axis=1, tiled=True)
    cross_part = lax.dot_general(instruments, targets, contract, preferred_element_type=jnp.float32)
    cross = lax.psum(cross_part, ("rows", "rhs")) / count
    coefficients = solve_with(factor, cross)
    fitted = jnp.dot(
        instruments, coefficients.astype(jnp.bfloat16), preferred_element_type=jnp.float32
    )
    return (coefficients, fitted)


def solution(mesh):
    placed = (P(("rows", "rhs"), None), P(), P(), P(), P("rows", "rhs"))
    return jax.shard_map(
        body, mesh=mesh, in_specs=placed, out_specs=(P(), P(("rows", "rhs"), None)), check_vma=False
    )
```

profile of v0, /device:TPU:0, one launch (start us, length us, event | category | flops | bytes accessed | tf_op | source)
XLA Modules:
  0.0 364.8 jit_solution(18324534306063840201)
XLA Ops:
  7.2 6.5 %all-to-all-start = ((bf16[4,2048,128]{2,1,0:T(8,128)(2,1)}), bf16[4,2048,128]{2,1,0:T(8,128)(2,1)S(1)}, u32[]{:S(2)}, u32[]{:S(2)}) async-start(bf16[4,2048,128]{2,1,0:T(8,128)(2,1)} %bitcast.66), calls=%async_computation | async-start | bytes 4194304 | tf_op jit(solution)/shard_map/all_to_all | solution.py:36
  13.7 1.9 copy.31
  15.7 2.6 gather_fusion
  18.3 17.9 %multiply_convert_fusion = bf16[512,2048]{1,0:T(8,128)(2,1)S(1)} fusion(f32[512,16]{1,0:T(8,128)S(1)} %gather_fusion, f32[2048,16]{0,1:T(8,128)S(1)} %copy-done, f32[512]{0:T(512)S(1)} %copy-done.8), kind=kOutput, calls=%fused_computation.3 | convolution fusion | flops 204472320 | bytes 2263040 | tf_op jit(solution)/shard_map/dot_general | solution.py:16
  37.6 2.3 fusion.50
  39.8 22.0 %all-to-all-done = bf16[4,2048,128]{2,1,0:T(8,128)(2,1)S(1)} async-done(((bf16[4,2048,128]{2,1,0:T(8,128)(2,1)}), bf16[4,2048,128]{2,1,0:T(8,128)(2,1)S(1)}, u32[]{:S(2)}, u32[]{:S(2)}) %all-to-all-start) | async-done | bytes 2097184 | tf_op jit(solution)/shard_map/all_to_all | solution.py:36
  61.9 3.1 copy.42
  65.0 4.5 %fusion.51 = f32[512,512]{0,1:T(8,128)} fusion(bf16[512,2048]{1,0:T(8,128)(2,1)} %copy-done.3, bf16[2048,512]{0,1:T(8,128)(2,1)} %bitcast.67), kind=kOutput, calls=%fused_computation.97 | convolution fusion | flops 1073741824 | bytes 5242880 | tf_op jit(solution)/shard_map/dot_general | solution.py:37
  69.5 133.9 %all-reduce.4.cloned.1.call-done = (f32[512,512]{0,1:T(8,128)}, f32[512,512]{0,1:T(8,128)}) async-done(((f32[512,512]{0,1:T(8,128)}, f32[512,512]{0,1:T(8,128)}), (f32[512,512]{0,1:T(8,128)}, f32[512,512]{0,1:T(8,128)})) %all-reduce.4.cloned.1.call-update) | async-done | bytes 2097168 | tf_op jit(solution)/shard_map/psum | solution.py:38
  203.4 2.8 select_add_fusion
  206.2 1.6 copy.33
  209.1 11.7 %cholesky.103 = f32[128,128]{1,0:T(8,128)S(1)} custom-call(f32[128,128]{1,0:T(8,128)S(1)} %cholesky.263), custom_call_target="Cholesky" | custom-call | tf_op jit(solution)/shard_map/jit(cholesky)/cholesky | solution.py:35
  220.9 9.8 %custom-call.32 = f32[1,128,128]{1,2,0:T(8,128)S(1)} custom-call(f32[1,128,128]{2,1,0:T(8,128)S(1)} %get-tuple-element.39), custom_call_target="InvertDiagBlocksLowerTriangular" | custom-call | tf_op jit(solution)/shard_map/jit(cholesky)/cholesky | solution.py:35
  233.4 11.9 %cholesky.215 = f32[128,128]{1,0:T(8,128)S(1)} custom-call(f32[128,128]{1,0:T(8,128)S(1)} %cholesky.267), custom_call_target="Cholesky" | custom-call | tf_op jit(solution)/shard_map/jit(cholesky)/cholesky | solution.py:35
  245.4 9.8 %custom-call.33 = f32[1,128,128]{1,2,0:T(8,128)S(1)} custom-call(f32[1,128,128]{2,1,0:T(8,128)S(1)} %get-tuple-element.37), custom_call_target="InvertDiagBlocksLowerTriangular" | custom-call | tf_op jit(solution)/shard_map/jit(cholesky)/cholesky | solution.py:35
  255.7 1.5 convolution_subtract_fusion.7
  257.2 11.7 %cholesky.236 = f32[128,128]{1,0:T(8,128)S(1)} custom-call(f32[128,128]{1,0:T(8,128)S(1)} %cholesky.272), custom_call_target="Cholesky" | custom-call | tf_op jit(solution)/shard_map/jit(cholesky)/cholesky | solution.py:35
  269.1 9.8 %custom-call.34 = f32[1,128,128]{1,2,0:T(8,128)S(1)} custom-call(f32[1,128,128]{2,1,0:T(8,128)S(1)} %get-tuple-element.35), custom_call_target="InvertDiagBlocksLowerTriangular" | custom-call | tf_op jit(solution)/shard_map/jit(cholesky)/cholesky | solution.py:35
  280.5 11.9 %cholesky.253 = f32[128,128]{1,0:T(8,128)S(1)} custom-call(f32[128,128]{1,0:T(8,128)S(1)} %convolution_subtract_fusion.8), custom_call_target="Cholesky" | custom-call | tf_op jit(solution)/shard_map/jit(cholesky)/cholesky | solution.py:35
  297.9 8.9 %while.1 = (s32[]{:T(128)}, f32[512,512]{0,1:T(8,128)S(1)}, s32[4,2]{0,1:T(2,128)S(1)}, f32[4,128,128]{2,1,0:T(8,128)S(1)}, s32[]{:T(128)}) while((s32[]{:T(128)}, f32[512,512]{0,1:T(8,128)S(1)}, s32[4,2]{0,1:T(2,128)S(1)}, f32[4,128,128]{2,1,0:T(8,128)S(1)}, s32[]{:T(128)}) %tuple.30), condition=%wide.while_cond, body=%wide.while_body.sunk | while | flops 2 | bytes 393329 | solution.py:11
  298.6 1.4 dynamic-slice.7
  306.8 39.3 %custom-call.35 = f32[4,128,128]{1,2,0:T(8,128)S(1)} custom-call(f32[4,128,128]{2,1,0:T(8,128)S(1)} %get-tuple-element.9), custom_call_target="InvertDiagBlocksLowerTriangular" | custom-call | tf_op jit(solution)/shard_map/triangular_solve | solution.py:11
  349.0 1.5 convolution_subtract_fusion.5
  354.4 3.3 fusion.17
  (86 shorter events, 24.7 us)
Async XLA Ops:
  7.2 11.2 %copy-start = (f32[2048,16]{0,1:T(8,128)S(1)}, f32[2048,16]{0,1:T(8,128)}, u32[]{:S(2)}) copy-start(f32[2048,16]{0,1:T(8,128)} %param.5) | copy-start | bytes 393220
  7.2 6.6 %copy-start.6 = (f32[4096,16]{0,1:T(8,128)S(1)}, f32[4096,16]{0,1:T(8,128)}, u32[]{:S(2)}) copy-start(f32[4096,16]{0,1:T(8,128)} %param.6) | copy-start | bytes 786436
  7.2 54.7 %all-to-all-start = ((bf16[4,2048,128]{2,1,0:T(8,128)(2,1)}), bf16[4,2048,128]{2,1,0:T(8,128)(2,1)S(1)}, u32[]{:S(2)}, u32[]{:S(2)}) async-start(bf16[4,2048,128]{2,1,0:T(8,128)(2,1)} %bitcast.66), calls=%async_computation | async-start | bytes 4194304 | tf_op jit(solution)/shard_map/all_to_all | solution.py:36
  13.7 2.0 copy-start.7
  13.7 4.6 %copy-start.8 = (f32[512]{0:T(512)S(1)}, f32[512]{0:T(512)}, u32[]{:S(2)}) copy-start(f32[512]{0:T(512)} %param.8) | copy-start | bytes 6148
  13.7 189.7 %all-reduce.4.cloned.1.call-start = ((), (), s32[]{:S(2)}) async-start(), calls=%async_computation.1 | async-start | bytes 4194304 | tf_op jit(solution)/shard_map/psum | solution.py:38
  36.2 1.3 copy-start.3
  206.2 1.7 copy-start.2
  208.1 1.0 copy-start.5
  352.8 1.6 copy-start.4
  354.4 3.3 copy-start.1
Sparse Core Ops, SparseCore 0:
  69.6 133.7 all-reduce.3
where the time goes:
time: 369 us; the launch traced here: 365 us
  waiting for transfers between devices  156 us (42%)
  other arithmetic  122 us (33%)
  matrix products  41.5 us (11%)
  local copies, waits for them, and re-layouts  21.6 us (6%)
  between operations  17.2 us (5%)
  starting transfers between devices  6.53 us (2%)
    psum x1, waiting for transfers between devices, body(): cross = lax.psum(cross_part, ('rows', 'rhs')) / count  134 us
    another operation x15, other arithmetic, body(): factor = jnp.linalg.cholesky(gram)  79.4 us
    another operation x4, other arithmetic, solve_with(): lax.linalg.triangular_solve(factor, lower, left_side=True, lower=True, tr...  39.5 us
    all_to_all x1, waiting for transfers between devices, body(): lax.all_to_all(treatment_features, 'rhs', split_axis=0, concat_axis=1, ti...  22 us
    dot_general x1, matrix products, features_of(): jnp.dot(values, freqs.T, precision=lax.Precision.HIGHEST, preferred_eleme...  17.9 us
    another operation x20, local copies, waits for them, and re-layouts  8.79 us
  transfers between devices with their start and end apart: 2, of which 2 were waited for; matrix products, arithmetic and copies ran while one was open for 7% of the time, Pallas kernels for 0%

commit v1 on v0

--- a/solution.py
+++ b/solution.py
@@ -35,7 +35,7 @@
     factor = jnp.linalg.cholesky(gram)
     targets = lax.all_to_all(treatment_features, "rhs", split_axis=0, concat_axis=1, tiled=True)
     cross_part = lax.dot_general(instruments, targets, contract, preferred_element_type=jnp.float32)
-    cross = lax.psum(cross_part, ("rows", "rhs")) / count
+    cross = lax.psum(lax.psum(cross_part, "rhs"), "rows") / count
     coefficients = solve_with(factor, cross)
     fitted = jnp.dot(
         instruments, coefficients.astype(jnp.bfloat16), preferred_element_type=jnp.float32

time: 369 us -> 402 us (1.089)
  waiting for transfers between devices: 156 us -> 177 us
    psum x1 -> x3, waiting for transfers between devices: 134 us -> 177 us  [the longest x1 136 us: body(): gram = lax.psum(gram_part, ('rows', 'rhs')) / count]
    all_to_all x1, waiting for transfers between devices: 22 us -> 0.01 us  [body(): lax.all_to_all(treatment_features, 'rhs', split_axis=0, concat_axis=1, ti...]
    another operation x15 -> x14, other arithmetic: 79.4 us -> 80.8 us  [body(): factor = jnp.linalg.cholesky(gram)]
  transfers between devices with their start and end apart: 2 -> 4, of which waited for: 2 -> 3; matrix products, arithmetic and copies ran while one was open for 7% -> 43% of each run, Pallas kernels for 0% -> 0%
where the time goes in v1:
time: 402 us; the launch traced here: 397 us
  waiting for transfers between devices  177 us (44%)
  other arithmetic  126 us (31%)
  matrix products  42.4 us (11%)
  local copies, waits for them, and re-layouts  25.5 us (6%)
  between operations  18.8 us (5%)
  starting transfers between devices  7.04 us (2%)
    psum x1, waiting for transfers between devices, body(): gram = lax.psum(gram_part, ('rows', 'rhs')) / count  136 us
    another operation x14, other arithmetic, body(): factor = jnp.linalg.cholesky(gram)  80.8 us
    psum x2, waiting for transfers between devices, body(): cross = lax.psum(lax.psum(cross_part, 'rhs'), 'rows') / count  40.8 us
    another operation x4, other arithmetic, solve_with(): lax.linalg.triangular_solve(factor, lower, left_side=True, lower=True, tr...  40.3 us
    dot_general x1, matrix products, features_of(): jnp.dot(values, freqs.T, precision=lax.Precision.HIGHEST, preferred_eleme...  17.9 us
    another operation x20, local copies, waits for them, and re-layouts  10.7 us
  transfers between devices with their start and end apart: 4, of which 3 were waited for; matrix products, arithmetic and copies ran while one was open for 43% of the time, Pallas kernels for 0%

profile of v1, /device:TPU:0, one launch (start us, length us, event | category | flops | bytes accessed | tf_op | source)
XLA Modules:
  0.0 397.3 jit_solution(9543491640993765369)
XLA Ops:
  8.0 6.5 %all-to-all-start = ((bf16[4,2048,128]{2,1,0:T(8,128)(2,1)}), bf16[4,2048,128]{2,1,0:T(8,128)(2,1)S(1)}, u32[]{:S(2)}, u32[]{:S(2)}) async-start(bf16[4,2048,128]{2,1,0:T(8,128)(2,1)} %bitcast.66), calls=%async_computation | async-start | bytes 4194304 | tf_op jit(solution)/shard_map/all_to_all | solution.py:36
  14.6 1.9 copy.31
  16.5 2.6 gather_fusion
  19.1 17.9 %multiply_convert_fusion = bf16[512,2048]{1,0:T(8,128)(2,1)S(1)} fusion(f32[512,16]{1,0:T(8,128)S(1)} %gather_fusion, f32[2048,16]{0,1:T(8,128)S(1)} %copy-done, f32[512]{0:T(512)S(1)} %copy-done.9), kind=kOutput, calls=%fused_computation.3 | convolution fusion | flops 204472320 | bytes 2263040 | tf_op jit(solution)/shard_map/dot_general | solution.py:16
  38.4 2.2 fusion.50
  41.2 136.1 %all-reduce.5.cloned.1.call-done = f32[512,512]{0,1:T(8,128)} async-done(((f32[512,512]{0,1:T(8,128)}), f32[512,512]{0,1:T(8,128)}) %all-reduce.5.cloned.1.call-update) | async-done | bytes 1048592 | tf_op jit(solution)/shard_map/psum | solution.py:33
  177.3 2.4 select_add_fusion
  179.8 2.6 copy.33
  182.3 1.5 fusion
  184.8 11.7 %cholesky.103 = f32[128,128]{1,0:T(8,128)S(1)} custom-call(f32[128,128]{1,0:T(8,128)S(1)} %cholesky.263), custom_call_target="Cholesky" | custom-call | tf_op jit(solution)/shard_map/jit(cholesky)/cholesky | solution.py:35
  196.7 9.8 %custom-call.32 = f32[1,128,128]{1,2,0:T(8,128)S(1)} custom-call(f32[1,128,128]{2,1,0:T(8,128)S(1)} %get-tuple-element.37), custom_call_target="InvertDiagBlocksLowerTriangular" | custom-call | tf_op jit(solution)/shard_map/jit(cholesky)/cholesky | solution.py:35
  209.1 11.7 %cholesky.215 = f32[128,128]{1,0:T(8,128)S(1)} custom-call(f32[128,128]{1,0:T(8,128)S(1)} %cholesky.267), custom_call_target="Cholesky" | custom-call | tf_op jit(solution)/shard_map/jit(cholesky)/cholesky | solution.py:35
  221.6 10.6 %custom-call.33 = f32[1,128,128]{1,2,0:T(8,128)} custom-call(f32[1,128,128]{2,1,0:T(8,128)S(1)} %get-tuple-element.35), custom_call_target="InvertDiagBlocksLowerTriangular" | custom-call | tf_op jit(solution)/shard_map/jit(cholesky)/cholesky | solution.py:35
  234.4 1.5 convolution_subtract_fusion.7
  235.9 11.7 %cholesky.236 = f32[128,128]{1,0:T(8,128)S(1)} custom-call(f32[128,128]{1,0:T(8,128)S(1)} %cholesky.272), custom_call_target="Cholesky" | custom-call | tf_op jit(solution)/shard_map/jit(cholesky)/cholesky | solution.py:35
  248.4 10.6 %custom-call.34 = f32[1,128,128]{1,2,0:T(8,128)S(1)} custom-call(f32[1,128,128]{2,1,0:T(8,128)} %get-tuple-element.33), custom_call_target="InvertDiagBlocksLowerTriangular" | custom-call | tf_op jit(solution)/shard_map/jit(cholesky)/cholesky | solution.py:35
  259.4 2.7 copy.42
  262.1 4.5 %fusion.51 = f32[512,512]{0,1:T(8,128)} fusion(bf16[512,2048]{1,0:T(8,128)(2,1)} %copy-done.3, bf16[2048,512]{0,1:T(8,128)(2,1)} %bitcast.67), kind=kOutput, calls=%fused_computation.97 | convolution fusion | flops 1073741824 | bytes 5242880 | tf_op jit(solution)/shard_map/dot_general | solution.py:37
  268.0 11.7 %cholesky.253 = f32[128,128]{1,0:T(8,128)S(1)} custom-call(f32[128,128]{1,0:T(8,128)S(1)} %convolution_subtract_fusion.8), custom_call_target="Cholesky" | custom-call | tf_op jit(solution)/shard_map/jit(cholesky)/cholesky | solution.py:35
  284.8 32.6 %all-reduce.7.cloned.1.call-done = f32[512,512]{0,1:T(8,128)} async-done(((f32[512,512]{0,1:T(8,128)}), f32[512,512]{0,1:T(8,128)}) %all-reduce.7.cloned.1.call-update) | async-done | bytes 1048592 | tf_op jit(solution)/shard_map/psum | solution.py:38
  317.4 10.9 %while.1 = (s32[]{:T(128)}, f32[512,512]{0,1:T(8,128)S(1)}, s32[4,2]{0,1:T(2,128)S(1)}, f32[4,128,128]{2,1,0:T(8,128)}, s32[]{:T(128)}) while((s32[]{:T(128)}, f32[512,512]{0,1:T(8,128)S(1)}, s32[4,2]{0,1:T(2,128)S(1)}, f32[4,128,128]{2,1,0:T(8,128)}, s32[]{:T(128)}) %tuple.30), condition=%wide.while_cond, body=%wide.while_body.sunk | while | flops 2 | bytes 393329 | solution.py:11
  328.3 40.1 %custom-call.35 = f32[4,128,128]{1,2,0:T(8,128)S(1)} custom-call(f32[4,128,128]{2,1,0:T(8,128)} %get-tuple-element.9), custom_call_target="InvertDiagBlocksLowerTriangular" | custom-call | tf_op jit(solution)/shard_map/triangular_solve | solution.py:11
  368.5 8.2 %all-reduce.9.cloned.1.call-done = f32[512,512]{0,1:T(8,128)} async-done(((f32[512,512]{0,1:T(8,128)}), f32[512,512]{0,1:T(8,128)}) %all-reduce.9.cloned.1.call-update) | async-done | bytes 1048592 | tf_op jit(solution)/shard_map/psum | solution.py:38
  386.3 3.3 fusion.17
  (94 shorter events, 33.6 us)
Async XLA Ops:
  8.0 11.1 %copy-start = (f32[2048,16]{0,1:T(8,128)S(1)}, f32[2048,16]{0,1:T(8,128)}, u32[]{:S(2)}) copy-start(f32[2048,16]{0,1:T(8,128)} %param.5) | copy-start | bytes 393220
  8.0 6.5 %copy-start.8 = (s32[512]{0:T(512)S(1)}, s32[512]{0:T(512)}, u32[]{:S(2)}) copy-start(s32[512]{0:T(512)} %param.7) | copy-start | bytes 6148
  8.0 6.5 %copy-start.7 = (f32[4096,16]{0,1:T(8,128)S(1)}, f32[4096,16]{0,1:T(8,128)}, u32[]{:S(2)}) copy-start(f32[4096,16]{0,1:T(8,128)} %param.6) | copy-start | bytes 786436
  8.0 251.3 %all-to-all-start = ((bf16[4,2048,128]{2,1,0:T(8,128)(2,1)}), bf16[4,2048,128]{2,1,0:T(8,128)(2,1)S(1)}, u32[]{:S(2)}, u32[]{:S(2)}) async-start(bf16[4,2048,128]{2,1,0:T(8,128)(2,1)} %bitcast.66), calls=%async_computation | async-start | bytes 4194304 | tf_op jit(solution)/shard_map/all_to_all | solution.py:36
  14.5 162.8 %all-reduce.5.cloned.1.call-start = ((), (), s32[]{:S(2)}) async-start(), calls=%async_computation.1 | async-start | bytes 2097152 | tf_op jit(solution)/shard_map/psum | solution.py:33
  14.6 4.6 %copy-start.9 = (f32[512]{0:T(512)S(1)}, f32[512]{0:T(512)}, u32[]{:S(2)}) copy-start(f32[512]{0:T(512)} %param.8) | copy-start | bytes 6148
  37.1 1.3 copy-start.3
  40.7 276.6 %all-reduce.7.cloned.1.call-start = ((), (), s32[]{:S(2)}) async-start(), calls=%async_computation.2 | async-start | bytes 2097152 | tf_op jit(solution)/shard_map/psum | solution.py:38
  177.3 5.0 %copy-start.1 = (f32[512,512]{0,1:T(8,128)S(1)}, f32[512,512]{0,1:T(8,128)}, u32[]{:S(2)}) copy-start(f32[512,512]{0,1:T(8,128)} %all-reduce.5.cloned.1.call-done) | copy-start | bytes 3145732
  183.8 1.0 copy-start.5
  209.1 12.5 %copy-start.6 = (f32[384,128]{1,0:T(8,128)}, f32[384,128]{1,0:T(8,128)S(1)}, u32[]{:S(2)}) copy-start(f32[384,128]{1,0:T(8,128)S(1)} %convolution_subtract_fusion.6) | copy-start | bytes 589828
  266.6 110.1 %all-reduce.9.cloned.1.call-start = ((), (), s32[]{:S(2)}) async-start(), calls=%async_computation.3 | async-start | bytes 2097152 | tf_op jit(solution)/shard_map/psum | solution.py:38
  384.7 1.6 copy-start.4
  386.3 3.3 copy-start.2
Sparse Core Ops, SparseCore 0:
  40.8 136.4 all-reduce.4
Sparse Core Ops, SparseCore 1:
  266.6 50.6 all-reduce.6
  320.4 56.3 all-reduce.8
